TPU v7x, 128 devices: a whole 4x4x4 slice. The times are simulated.
128 devices in a mesh: leaf: 16 (over x, y), side: 8 (over z, core).
Axes of the slice: x: 4, y: 4, z: 4, core: 2. Of those that a mesh axis runs over, the one named last changes fastest.
Arguments:
- block: float32 [131072, 512], P(('leaf', 'side')), may hold values from -24 to 24
- basis: float32 [131072, 1024], P(('leaf', 'side')), may hold values from -1 to 1
Outputs:
- ortho: float32 [131072, 512], P(('leaf', 'side'))
- factor: float32 [512, 512], replicated
- coeffs: float32 [1024, 512], replicated
All inputs are finite; a program needn't handle non-finite values.
Results may differ from a plain program's by a relative error of at most 0.0001.
Values sent between devices are 32-bit elements; how exact they have to be, the bound alone decides.
A program may use at most 64 MiB of HBM per device.

v0:
```python
import jax
import jax.numpy as jnp
from jax import lax
from jax.sharding import PartitionSpec as P


def inner(left, right):
    return lax.dot_general(
        left,
        right,
        (((0,), (0,)), ((), ())),
        precision=lax.Precision.HIGHEST,
        preferred_element_type=jnp.float32,
    )


def product(left, right):
    return jnp.dot(left, right, precision=lax.Precision.HIGHEST, preferred_element_type=jnp.float32)


def small_upper(matrix):
    width = matrix.shape[0]
    positions = jnp.arange(width, dtype=jnp.int32)

    def one_step(column, carry):
        rest, result = carry
        column = jnp.asarray(column).astype(jnp.int32)
        row = lax.dynamic_slice_in_dim(rest, column, 1, 0)[0]
        pivot = jnp.sqrt(jnp.sum(jnp.where(positions == column, row, jnp.float32(0.0))))
        new_row = jnp.where(positions >= column, row / pivot, jnp.float32(0.0))
        result = lax.dynamic_update_slice_in_dim(result, new_row[None, :], column, 0)
        rest = rest - new_row[:, None] * new_row[None, :]
        return (rest, result)

    start = (matrix, jnp.zeros_like(matrix))
    return lax.fori_loop(0, width, one_step, start)[1]


def small_inverse(upper_block):
    width = upper_block.shape[0]
    positions = jnp.arange(width, dtype=jnp.int32)

    def one_step(count, result):
        index = (width - 1 - jnp.asarray(count)).astype(jnp.int32)
        row = lax.dynamic_slice_in_dim(upper_block, index, 1, 0)[0]
        pivot = jnp.sum(jnp.where(positions == index, row, jnp.float32(0.0)))
        beyond = jnp.where(positions > index, row, jnp.float32(0.0))
        unit = jnp.where(positions == index, jnp.float32(1.0), jnp.float32(0.0))
        new_row = (unit - product(beyond[None, :], result)[0]) / pivot
        return lax.dynamic_update_slice_in_dim(result, new_row[None, :], index, 0)

    return lax.fori_loop(0, width, one_step, jnp.zeros_like(upper_block))


def factor_and_inverse(gram):
    width = gram.shape[0]
    piece = min(128, width)
    count = width // piece
    rest = gram
    strips = []
    diag_inverses = []
    for index in range(count):
        diag = small_upper(rest[:piece, :piece])
        diag_inv = small_inverse(diag)
        right = product(diag_inv.T, rest[:piece, piece:])
        left_zeros = jnp.zeros((piece, index * piece), gram.dtype)
        strips.append(jnp.concatenate([left_zeros, diag, right], axis=1))
        diag_inverses.append(diag_inv)
        rest = rest[piece:, piece:] - inner(right, right)
    factor = jnp.concatenate(strips, axis=0)
    lower_part = None
    for index in reversed(range(count)):
        diag_inv = diag_inverses[index]
        if lower_part is None:
            lower_part = diag_inv
        else:
            coupling = factor[index * piece : (index + 1) * piece, (index + 1) * piece :]
            far = -product(diag_inv, product(coupling, lower_part))
            top = jnp.concatenate([diag_inv, far], axis=1)
            below = jnp.concatenate(
                [jnp.zeros((lower_part.shape[0], piece), gram.dtype), lower_part], axis=1
            )
            lower_part = jnp.concatenate([top, below], axis=0)
    return (factor, lower_part)


def shards(block, basis):
    rows_total = block.shape[0] * lax.axis_size("leaf") * lax.axis_size("side")
    coeffs = lax.psum(inner(basis, block), ("leaf", "side"))
    projected = block - product(basis, coeffs)
    local_gram = inner(projected, projected) / rows_total
    factor, inverse = factor_and_inverse(lax.psum(local_gram, ("leaf", "side")))
    ortho = product(projected, inverse)
    return (ortho, factor, coeffs)


def solution(mesh):
    return jax.shard_map(
        shards,
        mesh=mesh,
        in_specs=(P(("leaf", "side"), None), P(("leaf", "side"), None)),
        out_specs=(P(("leaf", "side"), None), P(), P()),
        check_vma=False,
    )
```

profile of v0, /device:TPU:1, one launch (start us, length us, event | category | flops | bytes accessed | tf_op | source)
XLA Modules:
  0.0 1886.3 jit_solution(14410040137876746820)
XLA Ops:
  7.2 10.2 fusion.74
  17.7 1.3 copy-done
  19.0 1.8 copy.5
  20.8 150.3 %all-reduce.7.cloned.1.call-done = f32[1024,512]{1,0:T(8,128)} async-done(((f32[1024,512]{1,0:T(8,128)}), f32[1024,512]{1,0:T(8,128)}) %all-reduce.7.cloned.1.call-update) | async-done | bytes 2097168 | tf_op jit(solution)/shard_map/psum | solution.py:89
  171.2 16.2 bitcast_subtract_fusion
  187.3 4.5 convolution_multiply_fusion
  191.8 145.8 %all-reduce.9.cloned.1.call-done = f32[512,512]{1,0:T(8,128)} async-done(((f32[512,512]{1,0:T(8,128)}), f32[512,512]{1,0:T(8,128)}) %all-reduce.9.cloned.1.call-update) | async-done | bytes 1048592 | tf_op jit(solution)/shard_map/psum | solution.py:92
  337.6 0.8 slice.36
  338.5 192.5 %while.136 = (s32[]{:T(128)}, f32[128,128]{1,0:T(8,128)S(1)}, f32[128,128]{1,0:T(8,128)S(1)}, s32[]{:T(128)}, s32[]{:T(128)}) while((s32[]{:T(128)}, f32[128,128]{1,0:T(8,128)S(1)}, f32[128,128]{1,0:T(8,128)S(1)}, s32[]{:T(128)}, s32[]{:T(128)}) %tuple.273), condition=%wide.region_4.5_spmd.clone.clone, body=%wide.region_2.4_spmd.clone.clone.sunk | while | flops 34305 | bytes 142421 | solution.py:36
  531.0 187.3 %while.137 = (s32[]{:T(128)}, f32[128,128]{1,0:T(8,128)S(1)}, f32[128,128]{1,0:T(8,128)S(1)}, s32[]{:T(128)}, s32[]{:T(128)}, /*index=5*/s32[]{:T(128)}, s32[]{:T(128)}) while((s32[]{:T(128)}, f32[128,128]{1,0:T(8,128)S(1)}, f32[128,128]{1,0:T(8,128)S(1)}, s32[]{:T(128)}, s32[]{:T(128)}, /*index=5*/s32[]{:T(128)}, ...), condition=%wide.region_7.8_spmd.clone.clone, body=%wide.region_5.7_spmd.clone.clone.sunk | while | flops 197765 | bytes 69783 | solution.py:52
  531.6 0.8 fusion.139
  557.9 0.8 fusion.139
  559.4 0.8 fusion.139
  585.7 0.8 fusion.139
  587.1 0.8 fusion.139
  613.4 0.8 fusion.139
  614.9 0.8 fusion.139
  641.2 0.8 fusion.139
  642.7 0.8 fusion.139
  669.0 0.8 fusion.139
  670.4 0.8 fusion.139
  696.8 0.8 fusion.139
  698.2 0.8 fusion.139
  718.9 1.3 fusion.63
  720.2 1.7 convolution_subtract_fusion
  722.0 192.5 %while.138 = (s32[]{:T(128)}, f32[128,128]{1,0:T(8,128)S(1)}, f32[128,128]{1,0:T(8,128)S(1)}, s32[]{:T(128)}, s32[]{:T(128)}) while((s32[]{:T(128)}, f32[128,128]{1,0:T(8,128)S(1)}, f32[128,128]{1,0:T(8,128)S(1)}, s32[]{:T(128)}, s32[]{:T(128)}) %tuple.279), condition=%wide.region_10.11_spmd.clone.clone, body=%wide.region_8.10_spmd.clone.clone.sunk | while | flops 34305 | bytes 142421 | solution.py:36
  914.5 187.1 %while.139 = (s32[]{:T(128)}, f32[128,128]{1,0:T(8,128)S(1)}, f32[128,128]{1,0:T(8,128)S(1)}, s32[]{:T(128)}, s32[]{:T(128)}, /*index=5*/s32[]{:T(128)}, s32[]{:T(128)}) while((s32[]{:T(128)}, f32[128,128]{1,0:T(8,128)S(1)}, f32[128,128]{1,0:T(8,128)S(1)}, s32[]{:T(128)}, s32[]{:T(128)}, /*index=5*/s32[]{:T(128)}, ...), condition=%wide.region_13.14_spmd.clone.clone, body=%wide.region_11.13_spmd.clone.clone.sunk | while | flops 197765 | bytes 69783 | solution.py:52
  918.0 0.8 fusion.145
  919.5 0.8 fusion.145
  945.8 0.8 fusion.145
  947.2 0.8 fusion.145
  973.5 0.8 fusion.145
  975.0 0.8 fusion.145
  1001.3 0.8 fusion.145
  1002.8 0.8 fusion.145
  1029.1 0.8 fusion.145
  1030.5 0.8 fusion.145
  1056.9 0.8 fusion.145
  1058.3 0.8 fusion.145
  1084.6 0.8 fusion.145
  1086.1 0.8 fusion.145
  1102.9 192.5 %while.140 = (s32[]{:T(128)}, f32[128,128]{1,0:T(8,128)S(1)}, f32[128,128]{1,0:T(8,128)S(1)}, s32[]{:T(128)}, s32[]{:T(128)}) while((s32[]{:T(128)}, f32[128,128]{1,0:T(8,128)S(1)}, f32[128,128]{1,0:T(8,128)S(1)}, s32[]{:T(128)}, s32[]{:T(128)}) %tuple.285), condition=%wide.region_16.17_spmd.clone.clone, body=%wide.region_14.16_spmd.clone.clone.sunk | while | flops 34305 | bytes 142421 | solution.py:36
  1295.4 187.1 %while.141 = (s32[]{:T(128)}, f32[128,128]{1,0:T(8,128)S(1)}, f32[128,128]{1,0:T(8,128)S(1)}, s32[]{:T(128)}, s32[]{:T(128)}, /*index=5*/s32[]{:T(128)}, s32[]{:T(128)}) while((s32[]{:T(128)}, f32[128,128]{1,0:T(8,128)S(1)}, f32[128,128]{1,0:T(8,128)S(1)}, s32[]{:T(128)}, s32[]{:T(128)}, /*index=5*/s32[]{:T(128)}, ...), condition=%wide.region_19.20_spmd.clone.clone, body=%wide.region_17.19_spmd.clone.clone.sunk | while | flops 197765 | bytes 69783 | solution.py:52
  1304.8 0.8 fusion.151
  1306.3 0.8 fusion.151
  1332.6 0.8 fusion.151
  1334.0 0.8 fusion.151
  1360.4 0.8 fusion.151
  1361.8 0.8 fusion.151
  1388.1 0.8 fusion.151
  1389.6 0.8 fusion.151
  1415.9 0.8 fusion.151
  1417.4 0.8 fusion.151
  1443.7 0.8 fusion.151
  1445.1 0.8 fusion.151
  1471.4 0.8 fusion.151
  1483.7 192.5 %while.142 = (s32[]{:T(128)}, f32[128,128]{1,0:T(8,128)S(1)}, f32[128,128]{1,0:T(8,128)S(1)}, s32[]{:T(128)}, s32[]{:T(128)}) while((s32[]{:T(128)}, f32[128,128]{1,0:T(8,128)S(1)}, f32[128,128]{1,0:T(8,128)S(1)}, s32[]{:T(128)}, s32[]{:T(128)}) %tuple.291), condition=%wide.region_22.23_spmd.clone.clone, body=%wide.region_20.22_spmd.clone.clone.sunk | while | flops 34305 | bytes 142421 | solution.py:36
  1676.3 187.1 %while.143 = (s32[]{:T(128)}, f32[128,128]{1,0:T(8,128)S(1)}, f32[128,128]{1,0:T(8,128)S(1)}, s32[]{:T(128)}, s32[]{:T(128)}, /*index=5*/s32[]{:T(128)}, s32[]{:T(128)}) while((s32[]{:T(128)}, f32[128,128]{1,0:T(8,128)S(1)}, f32[128,128]{1,0:T(8,128)S(1)}, s32[]{:T(128)}, s32[]{:T(128)}, /*index=5*/s32[]{:T(128)}, ...), condition=%wide.region_25.26_spmd.clone.clone, body=%wide.region_23.25_spmd.clone.clone.sunk | while | flops 197765 | bytes 69783 | solution.py:52
  1865.1 1.4 fusion.73
  1866.7 1.4 convolution_negate_fusion
  1868.2 8.0 fusion.56
  1876.2 1.1 select_maximum_fusion
  1877.3 0.8 copy-done.1
  1878.1 1.3 copy.83
  (4617 shorter events, 1100.8 us)
Async XLA Ops:
  7.2 164.0 %all-reduce.7.cloned.1.call-start = ((), (), s32[]{:S(2)}) async-start(), calls=%async_computation | async-start | bytes 4194304 | tf_op jit(solution)/shard_map/psum | solution.py:89
  17.4 1.6 copy-start
  17.4 320.2 %all-reduce.9.cloned.1.call-start = ((), (), s32[]{:S(2)}) async-start(), calls=%async_computation.1 | async-start | bytes 2097152 | tf_op jit(solution)/shard_map/psum | solution.py:92
  718.3 0.6 copy-start.2
  1101.5 0.6 copy-start.4
  1482.5 0.6 copy-start.6
  1863.3 1.3 copy-start.8
  1868.1 8.1 copy-start.3
  1868.1 8.1 copy-start.5
  1868.2 8.1 copy-start.7
  1868.2 8.1 copy-start.9
  1876.2 2.0 copy-start.1
Sparse Core Ops, SparseCore 0:
  17.6 153.5 all-reduce.6
  192.0 145.6 all-reduce.8
where the time goes:
time: 1900 us; the launch traced here: 1890 us
  other arithmetic  685 us (36%)
  matrix products  455 us (24%)
  loops' own time  391 us (21%)
  waiting for transfers between devices  296 us (16%)
  local copies, waits for them, and re-layouts  43.5 us (2%)
    dot_general x523, matrix products, product(): jnp.dot(left, right, precision=lax.Precision.HIGHEST, preferred_element_t...  438 us
    another operation x4, loops' own time, small_upper(): return lax.fori_loop(0, width, one_step, start)[1]  377 us
    reduce_sum x512, other arithmetic, one_step(): pivot = jnp.sum(jnp.where(positions == index, row, jnp.float32(0.0)))  311 us
    reduce_sum x512, other arithmetic, one_step(): jnp.sum(jnp.where(positions == column, row, jnp.float32(0.0)))  310 us
    psum x1, waiting for transfers between devices, shards(): coeffs = lax.psum(inner(basis, block), ('leaf', 'side'))  150 us
    psum x1, waiting for transfers between devices, shards(): factor, inverse = factor_and_inverse(lax.psum(local_gram, ('leaf', 'side')))  146 us
    sub x512, other arithmetic, one_step(): rest = rest - new_row[:, None] * new_row[None, :]  42.1 us

commit v1 on v0

--- a/solution.py
+++ b/solution.py
@@ -86,7 +86,7 @@
 
 def shards(block, basis):
     rows_total = block.shape[0] * lax.axis_size("leaf") * lax.axis_size("side")
-    coeffs = lax.psum(inner(basis, block), ("leaf", "side"))
+    coeffs = lax.psum(lax.psum(inner(basis, block), "side"), "leaf")
     projected = block - product(basis, coeffs)
     local_gram = inner(projected, projected) / rows_total
     factor, inverse = factor_and_inverse(lax.psum(local_gram, ("leaf", "side")))

time: 1900 us -> 1910 us (level)
    psum x1 -> x2, waiting for transfers between devices: 150 us -> 159 us  [shards(): coeffs = lax.psum(lax.psum(inner(basis, block), 'side'), 'leaf')]
where the time goes in v1:
time: 1910 us; the launch traced here: 1900 us
  other arithmetic  685 us (36%)
  matrix products  455 us (24%)
  loops' own time  391 us (20%)
  waiting for transfers between devices  307 us (16%)
  local copies, waits for them, and re-layouts  42.2 us (2%)
    dot_general x523, matrix products, product(): jnp.dot(left, right, precision=lax.Precision.HIGHEST, preferred_element_t...  438 us
    another operation x4, loops' own time, small_upper(): return lax.fori_loop(0, width, one_step, start)[1]  377 us
    reduce_sum x512, other arithmetic, one_step(): pivot = jnp.sum(jnp.where(positions == index, row, jnp.float32(0.0)))  311 us
    reduce_sum x512, other arithmetic, one_step(): jnp.sum(jnp.where(positions == column, row, jnp.float32(0.0)))  310 us
    psum x2, waiting for transfers between devices, shards(): coeffs = lax.psum(lax.psum(inner(basis, block), 'side'), 'leaf')  159 us
    psum x1, waiting for transfers between devices, shards(): factor, inverse = factor_and_inverse(lax.psum(local_gram, ('leaf', 'side')))  148 us
    sub x512, other arithmetic, one_step(): rest = rest - new_row[:, None] * new_row[None, :]  42.1 us

profile of v1, /device:TPU:1, one launch (start us, length us, event | category | flops | bytes accessed | tf_op | source)
XLA Modules:
  0.0 1895.5 jit_solution(2541943813805869805)
XLA Ops:
  7.2 10.2 fusion.74
  17.5 67.3 %all-reduce.8.cloned.1.call-done = f32[1024,512]{1,0:T(8,128)} async-done(((f32[1024,512]{1,0:T(8,128)}), f32[1024,512]{1,0:T(8,128)}) %all-reduce.8.cloned.1.call-update) | async-done | bytes 2097168 | tf_op jit(solution)/shard_map/psum | solution.py:89
  85.1 1.8 copy.5
  86.9 91.6 %all-reduce.10.cloned.1.call-done = f32[1024,512]{1,0:T(8,128)} async-done(((f32[1024,512]{1,0:T(8,128)}), f32[1024,512]{1,0:T(8,128)}) %all-reduce.10.cloned.1.call-update) | async-done | bytes 2097168 | tf_op jit(solution)/shard_map/psum | solution.py:89
  178.5 16.2 bitcast_subtract_fusion
  194.6 4.5 convolution_multiply_fusion
  199.1 148.0 %all-reduce.12.cloned.1.call-done = f32[512,512]{1,0:T(8,128)} async-done(((f32[512,512]{1,0:T(8,128)}), f32[512,512]{1,0:T(8,128)}) %all-reduce.12.cloned.1.call-update) | async-done | bytes 1048592 | tf_op jit(solution)/shard_map/psum | solution.py:92
  347.2 0.8 slice.36
  348.0 192.5 %while.136 = (s32[]{:T(128)}, f32[128,128]{1,0:T(8,128)S(1)}, f32[128,128]{1,0:T(8,128)S(1)}, s32[]{:T(128)}, s32[]{:T(128)}) while((s32[]{:T(128)}, f32[128,128]{1,0:T(8,128)S(1)}, f32[128,128]{1,0:T(8,128)S(1)}, s32[]{:T(128)}, s32[]{:T(128)}) %tuple.273), condition=%wide.region_5.6_spmd.clone.clone, body=%wide.region_3.5_spmd.clone.clone.sunk | while | flops 34305 | bytes 142421 | solution.py:36
  540.5 187.3 %while.137 = (s32[]{:T(128)}, f32[128,128]{1,0:T(8,128)S(1)}, f32[128,128]{1,0:T(8,128)S(1)}, s32[]{:T(128)}, s32[]{:T(128)}, /*index=5*/s32[]{:T(128)}, s32[]{:T(128)}) while((s32[]{:T(128)}, f32[128,128]{1,0:T(8,128)S(1)}, f32[128,128]{1,0:T(8,128)S(1)}, s32[]{:T(128)}, s32[]{:T(128)}, /*index=5*/s32[]{:T(128)}, ...), condition=%wide.region_8.9_spmd.clone.clone, body=%wide.region_6.8_spmd.clone.clone.sunk | while | flops 197765 | bytes 69783 | solution.py:52
  552.8 0.8 fusion.139
  554.3 0.8 fusion.139
  580.6 0.8 fusion.139
  582.1 0.8 fusion.139
  608.4 0.8 fusion.139
  609.8 0.8 fusion.139
  636.1 0.8 fusion.139
  637.6 0.8 fusion.139
  663.9 0.8 fusion.139
  665.4 0.8 fusion.139
  691.7 0.8 fusion.139
  693.1 0.8 fusion.139
  719.5 0.8 fusion.139
  720.9 0.8 fusion.139
  728.4 1.3 fusion.63
  729.7 1.7 convolution_subtract_fusion
  731.5 192.5 %while.138 = (s32[]{:T(128)}, f32[128,128]{1,0:T(8,128)S(1)}, f32[128,128]{1,0:T(8,128)S(1)}, s32[]{:T(128)}, s32[]{:T(128)}) while((s32[]{:T(128)}, f32[128,128]{1,0:T(8,128)S(1)}, f32[128,128]{1,0:T(8,128)S(1)}, s32[]{:T(128)}, s32[]{:T(128)}) %tuple.279), condition=%wide.region_11.12_spmd.clone.clone, body=%wide.region_9.11_spmd.clone.clone.sunk | while | flops 34305 | bytes 142421 | solution.py:36
  924.0 187.1 %while.139 = (s32[]{:T(128)}, f32[128,128]{1,0:T(8,128)S(1)}, f32[128,128]{1,0:T(8,128)S(1)}, s32[]{:T(128)}, s32[]{:T(128)}, /*index=5*/s32[]{:T(128)}, s32[]{:T(128)}) while((s32[]{:T(128)}, f32[128,128]{1,0:T(8,128)S(1)}, f32[128,128]{1,0:T(8,128)S(1)}, s32[]{:T(128)}, s32[]{:T(128)}, /*index=5*/s32[]{:T(128)}, ...), condition=%wide.region_14.15_spmd.clone.clone, body=%wide.region_12.14_spmd.clone.clone.sunk | while | flops 197765 | bytes 69783 | solution.py:52
  939.2 0.8 fusion.145
  940.7 0.8 fusion.145
  967.0 0.8 fusion.145
  968.5 0.8 fusion.145
  994.8 0.8 fusion.145
  996.2 0.8 fusion.145
  1022.6 0.8 fusion.145
  1024.0 0.8 fusion.145
  1050.3 0.8 fusion.145
  1051.8 0.8 fusion.145
  1078.1 0.8 fusion.145
  1079.6 0.8 fusion.145
  1105.9 0.8 fusion.145
  1107.3 0.8 fusion.145
  1112.5 192.5 %while.140 = (s32[]{:T(128)}, f32[128,128]{1,0:T(8,128)S(1)}, f32[128,128]{1,0:T(8,128)S(1)}, s32[]{:T(128)}, s32[]{:T(128)}) while((s32[]{:T(128)}, f32[128,128]{1,0:T(8,128)S(1)}, f32[128,128]{1,0:T(8,128)S(1)}, s32[]{:T(128)}, s32[]{:T(128)}) %tuple.285), condition=%wide.region_17.18_spmd.clone.clone, body=%wide.region_15.17_spmd.clone.clone.sunk | while | flops 34305 | bytes 142421 | solution.py:36
  1305.0 187.1 %while.141 = (s32[]{:T(128)}, f32[128,128]{1,0:T(8,128)S(1)}, f32[128,128]{1,0:T(8,128)S(1)}, s32[]{:T(128)}, s32[]{:T(128)}, /*index=5*/s32[]{:T(128)}, s32[]{:T(128)}) while((s32[]{:T(128)}, f32[128,128]{1,0:T(8,128)S(1)}, f32[128,128]{1,0:T(8,128)S(1)}, s32[]{:T(128)}, s32[]{:T(128)}, /*index=5*/s32[]{:T(128)}, ...), condition=%wide.region_20.21_spmd.clone.clone, body=%wide.region_18.20_spmd.clone.clone.sunk | while | flops 197765 | bytes 69783 | solution.py:52
  1311.4 0.8 fusion.151
  1312.9 0.8 fusion.151
  1339.2 0.8 fusion.151
  1340.7 0.8 fusion.151
  1367.0 0.8 fusion.151
  1368.4 0.8 fusion.151
  1394.7 0.8 fusion.151
  1396.2 0.8 fusion.151
  1422.5 0.8 fusion.151
  1424.0 0.8 fusion.151
  1450.3 0.8 fusion.151
  1451.7 0.8 fusion.151
  1493.2 192.5 %while.142 = (s32[]{:T(128)}, f32[128,128]{1,0:T(8,128)S(1)}, f32[128,128]{1,0:T(8,128)S(1)}, s32[]{:T(128)}, s32[]{:T(128)}) while((s32[]{:T(128)}, f32[128,128]{1,0:T(8,128)S(1)}, f32[128,128]{1,0:T(8,128)S(1)}, s32[]{:T(128)}, s32[]{:T(128)}) %tuple.291), condition=%wide.region_23.24_spmd.clone.clone, body=%wide.region_21.23_spmd.clone.clone.sunk | while | flops 34305 | bytes 142421 | solution.py:36
  1685.8 187.1 %while.143 = (s32[]{:T(128)}, f32[128,128]{1,0:T(8,128)S(1)}, f32[128,128]{1,0:T(8,128)S(1)}, s32[]{:T(128)}, s32[]{:T(128)}, /*index=5*/s32[]{:T(128)}, s32[]{:T(128)}) while((s32[]{:T(128)}, f32[128,128]{1,0:T(8,128)S(1)}, f32[128,128]{1,0:T(8,128)S(1)}, s32[]{:T(128)}, s32[]{:T(128)}, /*index=5*/s32[]{:T(128)}, ...), condition=%wide.region_26.27_spmd.clone.clone, body=%wide.region_24.26_spmd.clone.clone.sunk | while | flops 197765 | bytes 69783 | solution.py:52
  1874.7 1.4 fusion.73
  1876.3 1.4 convolution_negate_fusion
  1877.7 8.0 fusion.56
  1885.8 1.1 select_maximum_fusion
  1886.9 0.8 copy-done.1
  1887.7 1.3 copy.84
  (4620 shorter events, 1100.8 us)
Async XLA Ops:
  7.2 77.7 %all-reduce.8.cloned.1.call-start = ((), (), s32[]{:S(2)}) async-start(), calls=%async_computation | async-start | bytes 4194304 | tf_op jit(solution)/shard_map/psum | solution.py:89
  17.4 67.7 %copy-start = (f32[1024,512]{1,0:T(8,128)S(1)}, f32[1024,512]{1,0:T(8,128)}, u32[]{:S(2)}) copy-start(f32[1024,512]{1,0:T(8,128)} %param.18) | copy-start | bytes 6291460
  17.4 161.0 %all-reduce.10.cloned.1.call-start = ((), (), s32[]{:S(2)}) async-start(), calls=%async_computation.1 | async-start | bytes 4194304 | tf_op jit(solution)/shard_map/psum | solution.py:89
  84.8 262.3 %all-reduce.12.cloned.1.call-start = ((), (), s32[]{:S(2)}) async-start(), calls=%async_computation.2 | async-start | bytes 2097152 | tf_op jit(solution)/shard_map/psum | solution.py:92
  727.8 0.6 copy-start.2
  1111.1 0.6 copy-start.4
  1492.0 0.6 copy-start.6
  1872.9 1.3 copy-start.8
  1877.7 8.1 copy-start.3
  1877.7 8.1 copy-start.5
  1877.7 8.1 copy-start.7
  1877.7 8.1 copy-start.9
  1885.7 2.0 copy-start.1
Sparse Core Ops, SparseCore 0:
  17.6 67.2 all-reduce.7
  88.1 90.2 all-reduce.9
  199.3 147.8 all-reduce.11
